TPU v7x, 128 devices: a whole 4x4x4 slice. The times are simulated.
128 devices in a mesh: req: 16 (over y, z), head: 8 (over x, core).
Axes of the slice: x: 4, y: 4, z: 4, core: 2. Of those that a mesh axis runs over, the one named last changes fastest.
Arguments:
- hidden: bfloat16 [2048, 6144], P('req'), may hold values from -15 to 15
- attn_norm_gain: float32 [6144], replicated, may hold values from 0.3 to 3
- attn_norm_bias: float32 [6144], replicated, may hold values from -4 to 4
- mlp_norm_gain: float32 [6144], replicated, may hold values from 0.3 to 3
- mlp_norm_bias: float32 [6144], replicated, may hold values from -4 to 4
- qkv_weight: bfloat16 [6144, 9216], P('req', 'head'), may hold values from -0.078125 to 0.078125
- qkv_bias: float32 [9216], P('head'), may hold values from -3 to 3
- out_weight: bfloat16 [3072, 6144], P('head', 'req'), may hold values from -0.625 to 0.625
- out_bias: float32 [6144], replicated, may hold values from -3 to 3
- up_weight: bfloat16 [6144, 12288], P('req', 'head'), may hold values from -0.078125 to 0.078125
- up_bias: float32 [12288], P('head'), may hold values from -3 to 3
- down_weight: bfloat16 [12288, 6144], P('head', 'req'), may hold values from -0.0546875 to 0.0546875
- down_bias: float32 [6144], replicated, may hold values from -3 to 3
- cache_keys: bfloat16 [16, 4096, 3072], P('req', None, 'head'), may hold values from -1300 to 1300
- cache_values: bfloat16 [16, 4096, 3072], P('req', None, 'head'), may hold values from -6 to 6
- cached_len: int32 [16], P('req'), may hold values from 128 to 4096, as said below
Outputs:
- hidden_out: bfloat16 [2048, 6144], P('req')
- new_keys: bfloat16 [16, 128, 3072], P('req', None, 'head')
- new_values: bfloat16 [16, 128, 3072], P('req', None, 'head')
Inputs may be any that keep to these rules, and one draw needn't show every extreme that they name: `cached_len`: each entry is 128 or 4096, and both values occur.
All inputs are finite; a program needn't handle non-finite values.
Results may differ from a plain program's by a relative error of at most 0.0085.
The roundings to bfloat16 on the way count: a program that leaves them out, or rounds other values in their place, can miss the bound.
Values may be sent and summed in bfloat16 or wider, within the bound.
A program may use at most 128 MiB of HBM per device.

v0:
```python
import math
import jax
import jax.numpy as jnp
from jax import lax
from jax.sharding import PartitionSpec as P

DH = 96
ROT = 24
NEW = 128
CACHE = 4096
KBLOCK = 512


def normalize(values, norm_gain, norm_shift):
    widened = values.astype(jnp.float32)
    center = jnp.mean(widened, axis=-1, keepdims=True)
    spread = jnp.mean(jnp.square(widened - center), axis=-1, keepdims=True)
    return ((widened - center) * lax.rsqrt(spread + 1e-05) * norm_gain + norm_shift).astype(
        jnp.bfloat16
    )


def rotate(values, position):
    halfway = ROT // 2
    exponent = jnp.arange(halfway, dtype=jnp.float32) * (2.0 / ROT)
    frequency = jnp.power(10000.0, -exponent)
    angle = position[:, None] * frequency[None, :]
    cosine = jnp.cos(angle)[:, None, :]
    sine_part = jnp.sin(angle)[:, None, :]
    lower_half = values[..., :halfway]
    upper_half = values[..., halfway:ROT]
    return jnp.concatenate(
        [
            lower_half * cosine - upper_half * sine_part,
            upper_half * cosine + lower_half * sine_part,
            values[..., ROT:],
        ],
        axis=-1,
    )


def attend_request(qkv_rows, keys_old, values_old, length, local_heads):
    scale_factor = 1.0 / math.sqrt(DH)
    split_rows = qkv_rows.reshape(NEW, local_heads, 3, DH)
    position = length.astype(jnp.float32) + jnp.arange(NEW, dtype=jnp.float32)
    queries = rotate(split_rows[:, :, 0], position).astype(jnp.bfloat16)
    key_new = rotate(split_rows[:, :, 1], position).astype(jnp.bfloat16)
    value_new = split_rows[:, :, 2].astype(jnp.bfloat16)
    query_index = jnp.arange(NEW, dtype=jnp.int32)
    fresh_scores = (
        jnp.einsum("qhd,khd->hqk", queries, key_new, preferred_element_type=jnp.float32)
        * scale_factor
    )
    fresh_scores = jnp.where(
        (query_index[None, :] <= query_index[:, None])[None], fresh_scores, -1e30
    )
    block_total = (length + KBLOCK - 1) // KBLOCK
    key_offsets = jnp.arange(KBLOCK, dtype=jnp.int32)

    def score_block(block_index, carry):
        score_store, highest = carry
        first_key = block_index * KBLOCK
        key_block = lax.dynamic_slice_in_dim(keys_old, first_key, KBLOCK, 0)
        block_scores = (
            jnp.einsum("qhd,khd->hqk", queries, key_block, preferred_element_type=jnp.float32)
            * scale_factor
        )
        block_scores = jnp.where(
            (first_key + key_offsets < length)[None, None, :], block_scores, -1e30
        )
        score_store = lax.dynamic_update_slice_in_dim(score_store, block_scores, first_key, 2)
        return (score_store, jnp.maximum(highest, jnp.max(block_scores, axis=-1)))

    empty_store = jnp.zeros((local_heads, NEW, CACHE), jnp.float32)
    score_store, highest = lax.fori_loop(
        0, block_total, score_block, (empty_store, jnp.max(fresh_scores, axis=-1))
    )
    fresh_weights = jnp.exp(fresh_scores - highest[..., None])

    def weigh_block(block_index, carry):
        mixed, denominator = carry
        first_key = block_index * KBLOCK
        block_scores = lax.dynamic_slice_in_dim(score_store, first_key, KBLOCK, 2)
        block_weights = jnp.exp(block_scores - highest[..., None])
        value_block = lax.dynamic_slice_in_dim(values_old, first_key, KBLOCK, 0)
        mixed = mixed + jnp.einsum(
            "hqk,khd->qhd",
            block_weights.astype(jnp.bfloat16),
            value_block,
            preferred_element_type=jnp.float32,
        )
        return (mixed, denominator + jnp.sum(block_weights, axis=-1))

    initial = (
        jnp.einsum(
            "hqk,khd->qhd",
            fresh_weights.astype(jnp.bfloat16),
            value_new,
            preferred_element_type=jnp.float32,
        ),
        jnp.sum(fresh_weights, axis=-1),
    )
    mixed, denominator = lax.fori_loop(0, block_total, weigh_block, initial)
    attended = (mixed / jnp.transpose(denominator)[:, :, None]).astype(jnp.bfloat16)
    width = local_heads * DH
    return (
        attended.reshape(NEW, width),
        key_new.reshape(NEW, width),
        value_new.reshape(NEW, width),
    )


def body(
    hidden,
    attn_norm_gain,
    attn_norm_bias,
    mlp_norm_gain,
    mlp_norm_bias,
    qkv_weight,
    qkv_bias,
    out_weight,
    out_bias,
    up_weight,
    up_bias,
    down_weight,
    down_bias,
    cache_keys,
    cache_values,
    cached_len,
):
    qkv_cols = qkv_weight.shape[1]
    local_heads = qkv_cols // (3 * DH)
    attn_normed = normalize(hidden, attn_norm_gain, attn_norm_bias)
    mlp_normed = normalize(hidden, mlp_norm_gain, mlp_norm_bias)
    attn_blocks, mlp_blocks = (
        lax.all_to_all(attn_normed, "req", split_axis=1, concat_axis=0, tiled=True),
        lax.all_to_all(mlp_normed, "req", split_axis=1, concat_axis=0, tiled=True),
    )
    qkv_term = jnp.dot(attn_blocks, qkv_weight, preferred_element_type=jnp.float32)
    up_term = jnp.dot(mlp_blocks, up_weight, preferred_element_type=jnp.float32)
    summed = lax.psum_scatter(
        jnp.concatenate([qkv_term, up_term], axis=1), "req", scatter_dimension=0, tiled=True
    )
    qkv_sum = summed[:, :qkv_cols]
    up_sum = summed[:, qkv_cols:]
    qkv = qkv_sum + qkv_bias
    units = jax.nn.gelu(up_sum + up_bias, approximate=True).astype(jnp.bfloat16)
    keys_old = cache_keys[0].reshape(CACHE, local_heads, DH)
    values_old = cache_values[0].reshape(CACHE, local_heads, DH)
    attended_rows, key_rows, value_rows = attend_request(
        qkv, keys_old, values_old, cached_len[0], local_heads
    )
    key_list = [key_rows]
    value_list = [value_rows]
    new_keys = jnp.stack(key_list, axis=0)
    new_values = jnp.stack(value_list, axis=0)
    joined = jnp.concatenate([attended_rows, units], axis=1)
    head_width = attended_rows.shape[1]
    shard_rows = lax.all_gather(joined, "req", axis=0, tiled=True)
    attention_part = jnp.dot(
        shard_rows[:, :head_width], out_weight, preferred_element_type=jnp.float32
    )
    partial_out = attention_part + jnp.dot(
        shard_rows[:, head_width:], down_weight, preferred_element_type=jnp.float32
    )
    bias_total = out_bias + down_bias
    spread_out = lax.all_to_all(partial_out, "req", split_axis=0, concat_axis=1, tiled=True)
    summed_out = lax.psum(spread_out, "head")
    result = (hidden.astype(jnp.float32) + summed_out + bias_total).astype(jnp.bfloat16)
    return (result, new_keys, new_values)


def solution(mesh):
    return jax.shard_map(
        body,
        mesh=mesh,
        in_specs=(
            P("req", None),
            P(),
            P(),
            P(),
            P(),
            P("req", "head"),
            P("head"),
            P("head", "req"),
            P(),
            P("req", "head"),
            P("head"),
            P("head", "req"),
            P(),
            P("req", None, "head"),
            P("req", None, "head"),
            P("req"),
        ),
        out_specs=(P("req", None), P("req", None, "head"), P("req", None, "head")),
        check_vma=False,
    )
```

profile of v0, /device:TPU:0, one launch (start us, length us, event | category | flops | bytes accessed | tf_op | source)
XLA Modules:
  0.0 498.3 jit_solution(11655447223252928488)
XLA Ops:
  7.2 2.0 copy.39
  9.2 0.8 convert_reduce_fusion
  10.1 0.8 fusion.24
  10.9 5.4 %fusion.21 = (bf16[128,6144]{0,1:T(8,128)(2,1)}, bf16[128,6144]{0,1:T(8,128)(2,1)S(1)}) fusion(bf16[128,6144]{0,1:T(8,128)(2,1)S(1)} %copy.39, f32[6144]{0:T(1024)S(1)} %copy-done.7, f32[6144]{0:T(1024)S(1)} %copy-done.8, f32[128]{0:T(128)S(1)} %add_rsqrt_fusion, f32[128]{0:T(128)S(1)} %broadcast_multiply_fusion, f32[6144]{0:T(1024)S(1)} %copy-done.9, ...), kind=kLoop, calls=%fused_computation.29 | loop fusion | flops 7077888 | bytes 4817920 | tf_op jit(solution)/shard_map/convert_element_type | solution.py:18
  16.4 30.6 %all_to_all.57 = bf16[128,16,384]{0,2,1:T(8,128)(2,1)} all-to-all(bf16[128,16,384]{0,2,1:T(8,128)(2,1)S(1)} %bitcast.67), channel_id=1, replica_groups=mesh['req'=16,'head'=8] {'req'}, dimensions={1} | all-to-all | bytes 3145728 | tf_op jit(solution)/shard_map/all_to_all | solution.py:137
  47.0 3.8 all-to-all-start
  50.9 2.6 copy.41
  53.5 19.9 %all-to-all-done = bf16[128,16,384]{0,2,1:T(8,128)(2,1)S(1)} async-done(((bf16[128,16,384]{0,2,1:T(8,128)(2,1)}), bf16[128,16,384]{0,2,1:T(8,128)(2,1)S(1)}, u32[]{:S(2)}, u32[]{:S(2)}) %all-to-all-start) | async-done | bytes 1572896 | tf_op jit(solution)/shard_map/all_to_all | solution.py:136
  73.4 1.1 copy-done.4
  74.6 1.9 copy.40
  76.5 5.1 %fusion.47 = f32[2048,1536]{0,1:T(8,128)S(1)} fusion(bf16[2048,384]{1,0:T(8,128)(2,1)} %bitcast.63, bf16[384,1536]{1,0:T(8,128)(2,1)S(1)} %copy-done), kind=kOutput, calls=%fused_computation.79 | convolution fusion | flops 2415919104 | bytes 15335424 | tf_op jit(solution)/shard_map/dot_general | solution.py:140
  81.6 2.8 fusion.46
  84.3 11.1 %pad_maximum_fusion = f32[2048,2688]{0,1:T(8,128)} fusion(f32[2048,1536]{0,1:T(8,128)S(1)} %fusion.47, f32[2048,1152]{0,1:T(8,128)S(1)} %fusion.46), kind=kLoop, calls=%fused_computation.18 | loop fusion | flops 5505024 | bytes 44040192 | tf_op jit(solution)/shard_map/concatenate | solution.py:142
  96.4 4.8 copy.45
  101.1 4.9 copy.47
  106.2 124.0 %reduce-scatter.2.cloned.1.call-done = f32[128,2688]{0,1:T(8,128)} async-done(((f32[2048,2688]{0,1:T(8,128)}), f32[128,2688]{0,1:T(8,128)}) %reduce-scatter.2.cloned.1.call-update) | async-done | bytes 1376272 | tf_op jit(solution)/shard_map/reduce_scatter | solution.py:141
  230.3 1.3 slice_add_fusion.1
  232.0 3.8 broadcast_in_dim.20
  235.7 3.0 while.26
  236.4 2.4 fusion.70
  239.0 3.4 while.25
  239.0 1.3 constant_dynamic-slice_fusion.2
  240.7 1.4 fusion.66
  242.5 1.5 fusion.36
  244.9 118.5 %all-gather.2.cloned.1.call-done = bf16[2048,1920]{0,1:T(8,128)(2,1)} async-done(((bf16[128,1920]{0,1:T(8,128)(2,1)}), bf16[2048,1920]{0,1:T(8,128)(2,1)}) %all-gather.2.cloned.1.call-update) | async-done | bytes 7864336 | tf_op jit(solution)/shard_map/all_gather | solution.py:159
  363.4 5.9 %fusion.14 = f32[2048,384]{1,0:T(8,128)S(1)} fusion(bf16[1536,384]{1,0:T(8,128)(2,1)} %param.31, bf16[2048,1920]{0,1:T(8,128)(2,1)} %all-gather.2.cloned.1.call-done), kind=kOutput, calls=%fused_computation.19 | convolution fusion | flops 2415919104 | bytes 10616832 | tf_op jit(solution)/shard_map/dot_general | solution.py:163
  369.3 2.6 convolution_add_fusion
  371.9 42.9 %all_to_all.58 = f32[16,128,384]{2,1,0:T(8,128)} all-to-all(f32[16,128,384]{2,1,0:T(8,128)S(1)} %bitcast.60), channel_id=1, replica_groups=mesh['req'=16,'head'=8] {'req'}, dimensions={0} | all-to-all | bytes 6291456 | tf_op jit(solution)/shard_map/all_to_all | solution.py:167
  414.9 3.6 copy.49
  420.7 65.2 %all-reduce.2.cloned.1.call-done = f32[128,6144]{0,1:T(8,128)} async-done(((f32[128,6144]{0,1:T(8,128)}), f32[128,6144]{0,1:T(8,128)}) %all-reduce.2.cloned.1.call-update) | async-done | bytes 3145744 | tf_op jit(solution)/shard_map/psum | solution.py:168
  485.9 3.3 fusion.26
  489.2 2.6 copy.50
  (61 shorter events, 5.6 us)
Async XLA Ops:
  7.2 69.3 %copy-start = (bf16[384,1536]{1,0:T(8,128)(2,1)S(1)}, bf16[384,1536]{1,0:T(8,128)(2,1)}, u32[]{:S(2)}) copy-start(bf16[384,1536]{1,0:T(8,128)(2,1)} %param.29) | copy-start | bytes 3538948
  7.2 3.7 copy-start.8
  7.2 3.7 copy-start.7
  7.2 3.7 copy-start.10
  7.2 3.7 copy-start.9
  9.2 7.2 %copy-start.2 = (bf16[128,6144]{0,1:T(8,128)(2,1)}, bf16[128,6144]{0,1:T(8,128)(2,1)S(1)}, u32[]{:S(2)}) copy-start(bf16[128,6144]{0,1:T(8,128)(2,1)S(1)} %copy.39) | copy-start | bytes 4718596
  47.0 26.4 %all-to-all-start = ((bf16[128,16,384]{0,2,1:T(8,128)(2,1)}), bf16[128,16,384]{0,2,1:T(8,128)(2,1)S(1)}, u32[]{:S(2)}, u32[]{:S(2)}) async-start(bf16[128,16,384]{0,2,1:T(8,128)(2,1)} %bitcast.66), calls=%async_computation | async-start | bytes 3145728 | tf_op jit(solution)/shard_map/all_to_all | solution.py:136
  50.9 179.4 %reduce-scatter.2.cloned.1.call-start = ((), (), s32[]{:S(2)}) async-start(), calls=%async_computation.4 | async-start | bytes 23396352 | tf_op jit(solution)/shard_map/reduce_scatter | solution.py:141
  73.4 1.1 copy-start.4
  76.4 5.1 %copy-start.5 = (bf16[384,1152]{1,0:T(8,128)(2,1)S(1)}, bf16[384,1152]{1,0:T(8,128)(2,1)}, u32[]{:S(2)}) copy-start(bf16[384,1152]{1,0:T(8,128)(2,1)} %param.25) | copy-start | bytes 2654212
  95.5 267.9 %all-gather.2.cloned.1.call-start = ((), (), s32[]{:S(2)}) async-start(), calls=%async_computation.5 | async-start | bytes 8355840 | tf_op jit(solution)/shard_map/all_gather | solution.py:159
  101.1 129.1 %copy-start.13 = (f32[1152]{0:T(1024)S(1)}, f32[1152]{0:T(1024)}, u32[]{:S(2)}) copy-start(f32[1152]{0:T(1024)} %param.26) | copy-start | bytes 13828
  239.0 3.5 copy-start.14
  244.8 124.5 %copy-start.6 = (bf16[384,384]{1,0:T(8,128)(2,1)S(1)}, bf16[384,384]{1,0:T(8,128)(2,1)}, u32[]{:S(2)}) copy-start(bf16[384,384]{1,0:T(8,128)(2,1)} %param.27) | copy-start | bytes 884740
  244.8 241.0 %all-reduce.2.cloned.1.call-start = ((), (), s32[]{:S(2)}) async-start(), calls=%async_computation.6 | async-start | bytes 6291456 | tf_op jit(solution)/shard_map/psum | solution.py:168
  418.4 0.7 copy-start.11
  418.4 0.8 copy-start.12
  418.4 67.5 %copy-start.3 = (bf16[128,6144]{0,1:T(8,128)(2,1)S(1)}, bf16[128,6144]{0,1:T(8,128)(2,1)}, u32[]{:S(2)}) copy-start(bf16[128,6144]{0,1:T(8,128)(2,1)} %copy-done.2) | copy-start | bytes 4718596
  485.9 5.9 %copy-start.1 = (bf16[384,1536]{1,0:T(8,128)(2,1)S(1)}, bf16[384,1536]{1,0:T(8,128)(2,1)}, u32[]{:S(2)}) copy-start(bf16[384,1536]{1,0:T(8,128)(2,1)} %param.29) | copy-start | bytes 3538948
Sparse Core Ops, SparseCore 0:
  95.6 134.6 reduce-scatter.1
  244.9 118.4 all-gather.1
  418.6 67.2 all-reduce.1
where the time goes:
time: 500 us; the launch traced here: 498 us
  waiting for transfers between devices  328 us (66%)
  blocking collectives  73.5 us (15%)
  local copies, waits for them, and re-layouts  31.2 us (6%)
  other arithmetic  26.5 us (5%)
  matrix products  20.5 us (4%)
  between operations  14.7 us (3%)
    reduce_scatter x1, waiting for transfers between devices, body(): lax.psum_scatter(jnp.concatenate([qkv_term, up_term], axis=1), 'req', sca...  124 us
    all_gather x1, waiting for transfers between devices, body(): shard_rows = lax.all_gather(joined, 'req', axis=0, tiled=True)  119 us
    psum x1, waiting for transfers between devices, body(): summed_out = lax.psum(spread_out, 'head')  65.2 us
    all_to_all x1, blocking collectives, body(): lax.all_to_all(partial_out, 'req', split_axis=0, concat_axis=1, tiled=True)  42.9 us
    all_to_all x1, blocking collectives, body(): lax.all_to_all(mlp_normed, 'req', split_axis=1, concat_axis=0, tiled=True)  30.6 us
    all_to_all x1, waiting for transfers between devices, body(): lax.all_to_all(attn_normed, 'req', split_axis=1, concat_axis=0, tiled=True)  19.9 us
    unnamed x36, local copies, waits for them, and re-layouts  17.7 us
    concatenate x1, other arithmetic, body(): jnp.concatenate([qkv_term, up_term], axis=1)  11.1 us
  transfers between devices with their start and end apart: 4, of which 4 were waited for; matrix products, arithmetic and copies ran while one was open for 3% of the time, Pallas kernels for 0%

commit v1 on v0

--- a/solution.py
+++ b/solution.py
@@ -165,7 +165,11 @@
     )
     bias_total = out_bias + down_bias
     spread_out = lax.all_to_all(partial_out, "req", split_axis=0, concat_axis=1, tiled=True)
-    summed_out = lax.psum(spread_out, "head")
+    summed_out = spread_out
+    for hop in (1, 2, 4):
+        summed_out = summed_out + lax.ppermute(
+            summed_out, "head", [(dev, dev ^ hop) for dev in range(8)]
+        )
     result = (hidden.astype(jnp.float32) + summed_out + bias_total).astype(jnp.bfloat16)
     return (result, new_keys, new_values)
 

time: 500 us -> 585 us (1.17)
  waiting for transfers between devices: 328 us -> 404 us
    ppermute x0 -> x3, waiting for transfers between devices: none -> 141 us  [body(): lax.ppermute(summed_out, 'head', [(dev, dev ^ hop) for dev in range(8)])]
    psum x1 -> x0, waiting for transfers between devices: 65.2 us -> none  [body(): summed_out = lax.psum(spread_out, 'head')]
  transfers between devices with their start and end apart: 4 -> 6, of which waited for: 4 -> 6; matrix products, arithmetic and copies ran while one was open for 3% -> 2% of each run, Pallas kernels for 0% -> 0%
where the time goes in v1:
time: 585 us; the launch traced here: 584 us
  waiting for transfers between devices  404 us (69%)
  blocking collectives  73.5 us (13%)
  other arithmetic  31.6 us (5%)
  local copies, waits for them, and re-layouts  30.6 us (5%)
  matrix products  20.5 us (4%)
  between operations  15 us (3%)
  starting transfers between devices  8.64 us (1%)
    ppermute x3, waiting for transfers between devices, body(): lax.ppermute(summed_out, 'head', [(dev, dev ^ hop) for dev in range(8)])  141 us
    reduce_scatter x1, waiting for transfers between devices, body(): lax.psum_scatter(jnp.concatenate([qkv_term, up_term], axis=1), 'req', sca...  124 us
    all_gather x1, waiting for transfers between devices, body(): shard_rows = lax.all_gather(joined, 'req', axis=0, tiled=True)  119 us
    all_to_all x1, blocking collectives, body(): lax.all_to_all(partial_out, 'req', split_axis=0, concat_axis=1, tiled=True)  42.9 us
    all_to_all x1, blocking collectives, body(): lax.all_to_all(mlp_normed, 'req', split_axis=1, concat_axis=0, tiled=True)  30.6 us
    all_to_all x1, waiting for transfers between devices, body(): lax.all_to_all(attn_normed, 'req', split_axis=1, concat_axis=0, tiled=True)  19.9 us
    unnamed x36, local copies, waits for them, and re-layouts  17 us
  transfers between devices with their start and end apart: 6, of which 6 were waited for; matrix products, arithmetic and copies ran while one was open for 2% of the time, Pallas kernels for 0%

profile of v1, /device:TPU:0, one launch (start us, length us, event | category | flops | bytes accessed | tf_op | source)
XLA Modules:
  0.0 583.6 jit_solution(3998641433415657416)
XLA Ops:
  7.2 2.0 copy.39
  10.9 5.4 fusion.21
  16.4 30.6 %all_to_all.57 = bf16[128,16,384]{0,2,1:T(8,128)(2,1)} all-to-all(bf16[128,16,384]{0,2,1:T(8,128)(2,1)S(1)} %bitcast.68), channel_id=1, replica_groups=mesh['req'=16,'head'=8] {'req'}, dimensions={1} | all-to-all | bytes 3145728 | tf_op jit(solution)/shard_map/all_to_all | solution.py:137
  47.0 3.8 all-to-all-start
  50.9 2.6 copy.41
  53.5 19.9 %all-to-all-done = bf16[128,16,384]{0,2,1:T(8,128)(2,1)S(1)} async-done(((bf16[128,16,384]{0,2,1:T(8,128)(2,1)}), bf16[128,16,384]{0,2,1:T(8,128)(2,1)S(1)}, u32[]{:S(2)}, u32[]{:S(2)}) %all-to-all-start) | async-done | bytes 1572896 | tf_op jit(solution)/shard_map/all_to_all | solution.py:136
  74.6 1.9 copy.40
  76.5 5.1 fusion.47
  81.6 2.8 fusion.46
  84.3 11.1 %pad_maximum_fusion = f32[2048,2688]{0,1:T(8,128)} fusion(f32[2048,1536]{0,1:T(8,128)S(1)} %fusion.47, f32[2048,1152]{0,1:T(8,128)S(1)} %fusion.46), kind=kLoop, calls=%fused_computation.18 | loop fusion | flops 5505024 | bytes 44040192 | tf_op jit(solution)/shard_map/concatenate | solution.py:142
  96.4 4.8 copy.45
  101.2 4.9 copy.47
  106.3 124.0 %reduce-scatter.2.cloned.1.call-done = f32[128,2688]{0,1:T(8,128)} async-done(((f32[2048,2688]{0,1:T(8,128)}), f32[128,2688]{0,1:T(8,128)}) %reduce-scatter.2.cloned.1.call-update) | async-done | bytes 1376272 | tf_op jit(solution)/shard_map/reduce_scatter | solution.py:141
  232.0 3.8 broadcast_in_dim.20
  235.8 3.0 while.26
  236.4 2.4 fusion.70
  239.0 3.4 while.25
  242.5 1.5 fusion.36
  244.9 118.6 %all-gather.2.cloned.1.call-done = bf16[2048,1920]{0,1:T(8,128)(2,1)} async-done(((bf16[128,1920]{0,1:T(8,128)(2,1)}), bf16[2048,1920]{0,1:T(8,128)(2,1)}) %all-gather.2.cloned.1.call-update) | async-done | bytes 7864336 | tf_op jit(solution)/shard_map/all_gather | solution.py:159
  363.5 5.9 %fusion.14 = f32[2048,384]{1,0:T(8,128)S(1)} fusion(bf16[1536,384]{1,0:T(8,128)(2,1)} %param.31, bf16[2048,1920]{0,1:T(8,128)(2,1)} %all-gather.2.cloned.1.call-done), kind=kOutput, calls=%fused_computation.19 | convolution fusion | flops 2415919104 | bytes 10616832 | tf_op jit(solution)/shard_map/dot_general | solution.py:163
  369.4 2.6 convolution_add_fusion
  372.0 42.9 %all_to_all.58 = f32[16,128,384]{2,1,0:T(8,128)} all-to-all(f32[16,128,384]{2,1,0:T(8,128)S(1)} %bitcast.61), channel_id=1, replica_groups=mesh['req'=16,'head'=8] {'req'}, dimensions={0} | all-to-all | bytes 6291456 | tf_op jit(solution)/shard_map/all_to_all | solution.py:167
  415.0 3.6 copy.49
  418.5 5.9 %collective-permute-done = f32[128,6144]{0,1:T(8,128)S(1)} collective-permute-done((f32[128,6144]{0,1:T(8,128)}, f32[128,6144]{0,1:T(8,128)S(1)}, u32[]{:S(2)}, u32[]{:S(2)}) %collective-permute-start) | collective-permute-done | bytes 3145760 | tf_op jit(solution)/shard_map/ppermute | solution.py:170
  424.4 2.2 bitcast_add_fusion
  426.6 1.6 collective-permute-start.1
  428.2 68.7 %collective-permute-done.1 = f32[128,6144]{0,1:T(8,128)S(1)} collective-permute-done((f32[128,6144]{0,1:T(8,128)S(1)}, f32[128,6144]{0,1:T(8,128)S(1)}, u32[]{:S(2)}, u32[]{:S(2)}) %collective-permute-start.1) | collective-permute-done | bytes 3145760 | tf_op jit(solution)/shard_map/ppermute | solution.py:170
  496.9 2.0 add.147
  498.8 3.0 collective-permute-start.2
  503.3 66.6 %collective-permute-done.2 = f32[128,6144]{0,1:T(8,128)} collective-permute-done((f32[128,6144]{0,1:T(8,128)}, f32[128,6144]{0,1:T(8,128)}, u32[]{:S(2)}, u32[]{:S(2)}) %collective-permute-start.2) | collective-permute-done | bytes 3145760 | tf_op jit(solution)/shard_map/ppermute | solution.py:170
  569.9 4.3 fusion.26
  574.2 2.6 copy.50
  (66 shorter events, 11.7 us)
Async XLA Ops:
  7.2 69.3 %copy-start = (bf16[384,1536]{1,0:T(8,128)(2,1)S(1)}, bf16[384,1536]{1,0:T(8,128)(2,1)}, u32[]{:S(2)}) copy-start(bf16[384,1536]{1,0:T(8,128)(2,1)} %param.29) | copy-start | bytes 3538948
  7.2 3.7 copy-start.8
  7.2 3.7 copy-start.7
  7.2 3.7 copy-start.10
  7.2 3.7 copy-start.9
  9.2 7.2 %copy-start.2 = (bf16[128,6144]{0,1:T(8,128)(2,1)}, bf16[128,6144]{0,1:T(8,128)(2,1)S(1)}, u32[]{:S(2)}) copy-start(bf16[128,6144]{0,1:T(8,128)(2,1)S(1)} %copy.39) | copy-start | bytes 4718596
  47.0 26.4 %all-to-all-start = ((bf16[128,16,384]{0,2,1:T(8,128)(2,1)}), bf16[128,16,384]{0,2,1:T(8,128)(2,1)S(1)}, u32[]{:S(2)}, u32[]{:S(2)}) async-start(bf16[128,16,384]{0,2,1:T(8,128)(2,1)} %bitcast.67), calls=%async_computation | async-start | bytes 3145728 | tf_op jit(solution)/shard_map/all_to_all | solution.py:136
  50.9 179.4 %reduce-scatter.2.cloned.1.call-start = ((), (), s32[]{:S(2)}) async-start(), calls=%async_computation.4 | async-start | bytes 23396352 | tf_op jit(solution)/shard_map/reduce_scatter | solution.py:141
  73.4 1.1 copy-start.4
  76.4 5.1 copy-start.5
  95.5 268.0 %all-gather.2.cloned.1.call-start = ((), (), s32[]{:S(2)}) async-start(), calls=%async_computation.5 | async-start | bytes 8355840 | tf_op jit(solution)/shard_map/all_gather | solution.py:159
  101.2 129.1 %copy-start.13 = (f32[1152]{0:T(1024)S(1)}, f32[1152]{0:T(1024)}, u32[]{:S(2)}) copy-start(f32[1152]{0:T(1024)} %param.26) | copy-start | bytes 13828
  239.0 3.5 copy-start.14
  244.9 124.5 %copy-start.6 = (bf16[384,384]{1,0:T(8,128)(2,1)S(1)}, bf16[384,384]{1,0:T(8,128)(2,1)}, u32[]{:S(2)}) copy-start(bf16[384,384]{1,0:T(8,128)(2,1)} %param.27) | copy-start | bytes 884740
  418.5 5.9 %collective-permute-start = (f32[128,6144]{0,1:T(8,128)}, f32[128,6144]{0,1:T(8,128)S(1)}, u32[]{:S(2)}, u32[]{:S(2)}) collective-permute-start(f32[128,6144]{0,1:T(8,128)} %bitcast.60), channel_id=1, source_target_pairs={{0,1},{1,0},{2,3},{3,2},{4,5},{5,4},{6,7},{7,6},{8,9},{9,8},{10,11... | collective-permute-start | bytes 9437192 | tf_op jit(solution)/shard_map/ppermute | solution.py:170
  426.6 75.2 %copy-start.11 = (f32[6144]{0:T(1024)S(1)}, f32[6144]{0:T(1024)}, u32[]{:S(2)}) copy-start(f32[6144]{0:T(1024)} %param.28) | copy-start | bytes 73732
  426.6 75.2 %copy-start.12 = (f32[6144]{0:T(1024)S(1)}, f32[6144]{0:T(1024)}, u32[]{:S(2)}) copy-start(f32[6144]{0:T(1024)} %param.32) | copy-start | bytes 73732
  426.6 143.3 %copy-start.3 = (bf16[128,6144]{0,1:T(8,128)(2,1)S(1)}, bf16[128,6144]{0,1:T(8,128)(2,1)}, u32[]{:S(2)}) copy-start(bf16[128,6144]{0,1:T(8,128)(2,1)} %copy-done.2) | copy-start | bytes 4718596
  426.6 70.2 %collective-permute-start.1 = (f32[128,6144]{0,1:T(8,128)S(1)}, f32[128,6144]{0,1:T(8,128)S(1)}, u32[]{:S(2)}, u32[]{:S(2)}) collective-permute-start(f32[128,6144]{0,1:T(8,128)S(1)} %bitcast_add_fusion), channel_id=1, source_target_pairs={{0,2},{1,3},{2,0},{3,1},{4,6},{5,7},{6,4},{7,5},{8,10},{9,11},{10,... | collective-permute-start | bytes 9437192 | tf_op jit(solution)/shard_map/ppermute | solution.py:170
  498.8 71.1 %collective-permute-start.2 = (f32[128,6144]{0,1:T(8,128)}, f32[128,6144]{0,1:T(8,128)}, u32[]{:S(2)}, u32[]{:S(2)}) collective-permute-start(f32[128,6144]{0,1:T(8,128)} %add.147), channel_id=1, source_target_pairs={{0,4},{1,5},{2,6},{3,7},{4,0},{5,1},{6,2},{7,3},{8,12},{9,13},{10,... | collective-permute-start | bytes 9437192 | tf_op jit(solution)/shard_map/ppermute | solution.py:170
  569.9 6.9 %copy-start.1 = (bf16[384,1536]{1,0:T(8,128)(2,1)S(1)}, bf16[384,1536]{1,0:T(8,128)(2,1)}, u32[]{:S(2)}) copy-start(bf16[384,1536]{1,0:T(8,128)(2,1)} %param.29) | copy-start | bytes 3538948
Sparse Core Ops, SparseCore 0:
  95.6 134.6 reduce-scatter.1
  245.0 118.4 all-gather.1
